TPU v7x, 32 devices: a whole 2x2x4 slice. The times are simulated.
32 devices in a mesh: gz: 2 (over y), row: 4 (over x, core), col: 4 (over z).
Axes of the slice: x: 2, y: 2, z: 4, core: 2. Of those that a mesh axis runs over, the one named last changes fastest.
Arguments:
- anc_lower: bfloat16 [1, 1024, 1024], P(None, 'col', 'row'), may hold values from -0.125 to 0.125
- anc_upper: bfloat16 [1, 1024, 1024], P(None, 'col', 'row'), may hold values from -0.125 to 0.125
- sub_lower: bfloat16 [16, 1024, 1024], P('gz', 'col', 'row'), may hold values from -0.125 to 0.125
- sub_upper: bfloat16 [16, 1024, 1024], P('gz', 'col', 'row'), may hold values from -0.125 to 0.125
- anc_rhs: bfloat16 [1, 1024, 64], P(None, 'col'), may hold values from -6 to 6
- sub_rhs: bfloat16 [6, 1024, 64], P('gz', 'col'), may hold values from -6 to 6
- layer_subtree: int32 [2], replicated, may hold values from 0 to 1, each once
- sub_pattern: int32 [10, 2], P('gz'), may hold values 0 or 1
Outputs:
- anc_solution: float32 [1, 1024, 64], P(None, ('row', 'col'))
- sub_solution: float32 [6, 1024, 64], P('gz', ('row', 'col'))
Inputs may be any that keep to these rules, and one draw needn't show every extreme that they name: `layer_subtree`: each subtree is held by exactly one layer.
All inputs are finite; a program needn't handle non-finite values. No bound on the sum of `sub_pattern` on one device may be relied on, other than what follows from the above.
Results may differ from a plain program's by a relative error of at most 0.018.
Values may be sent and summed in bfloat16 or wider, within the bound.
A program may use at most 64 MiB of HBM per device.

v0:
```python
import jax
import jax.numpy as jnp
import numpy as np
from jax import lax
from jax.sharding import PartitionSpec as P

R = 64
SUB_LEVELS = 2
SUB_NODES = 3


def level_span(depth_now):
    return (2**depth_now - 1, 2 ** (depth_now + 1) - 1)


def local_routes(first_id, stop_id, depth_now, target_count):
    table = np.zeros((target_count, (stop_id - first_id) * depth_now), np.float32)
    for offset, member in enumerate(range(first_id, stop_id)):
        for local_level in range(depth_now):
            target = (member + 1 >> depth_now - local_level) - 1
            table[target, offset * depth_now + local_level] = 1.0
    return table


def solve_diagonal(residual, blocks):
    whole_blocks = lax.all_gather(blocks, "col", axis=1, tiled=True)
    whole_res = lax.all_gather(residual, "col", axis=1, tiled=True)
    rows_full = jnp.einsum(
        "nki,nkr->nir", whole_blocks, whole_res, preferred_element_type=jnp.float32
    )
    share = rows_full.shape[1] // lax.axis_size("col")
    owned = lax.dynamic_slice_in_dim(rows_full, lax.axis_index("col") * share, share, 1)
    return (owned, rows_full.astype(jnp.bfloat16))


def upper_sum(values):
    return lax.psum(values, "row")


def local(anc_lower, anc_upper, sub_lower, sub_upper, anc_rhs, sub_rhs, layer_subtree, sub_pattern):
    layers = lax.axis_size("gz")
    levels = layers.bit_length() - 1
    anc_count = layers - 1
    row_count = lax.axis_size("row")
    col_count = lax.axis_size("col")
    rows_here = anc_lower.shape[2]
    cols_here = anc_lower.shape[1]
    sub_start = [0]
    for member in range(SUB_NODES):
        sub_start.append(sub_start[-1] + levels + (member + 1).bit_length() - 1)
    anc_start = [0]
    for member in range(anc_count):
        anc_start.append(anc_start[-1] + (member + 1).bit_length() - 1)
    low_pattern = sub_pattern[:, 0].astype(jnp.float32)
    up_pattern = sub_pattern[:, 1].astype(jnp.float32)
    layer_here = lax.axis_index("gz")
    subtree = jnp.sum(
        jnp.where(jnp.arange(layers, dtype=jnp.int32) == layer_here, layer_subtree, 0)
    )
    powers = jnp.asarray(2 ** (levels - np.arange(levels)), jnp.int32)
    heap_ids = (subtree + layers) // powers - 1
    choose = (heap_ids[:, None] == jnp.arange(anc_count, dtype=jnp.int32)[None, :]).astype(
        jnp.float32
    )
    first_layer = (layer_here == 0).astype(jnp.float32)
    row_index = lax.axis_index("row")
    col_index = lax.axis_index("col")
    holds_piece = (row_index == col_index * row_count // col_count).astype(jnp.float32)
    piece_start = jnp.clip(col_index * cols_here - row_index * rows_here, 0, rows_here - cols_here)

    def own_piece(rows_block):
        return holds_piece * lax.dynamic_slice_in_dim(rows_block, piece_start, cols_here, 1).astype(
            jnp.float32
        )

    sub_acc = jnp.zeros((SUB_NODES, cols_here, R), jnp.float32)
    to_anc = jnp.zeros((anc_count, cols_here, R), jnp.float32)
    sub_rows = {}
    for depth_now in reversed(range(SUB_LEVELS)):
        first_id, stop_id = level_span(depth_now)
        node_count = stop_id - first_id
        given = sub_rhs[first_id:stop_id].astype(jnp.float32)
        if depth_now + 1 < SUB_LEVELS:
            given = given - lax.psum(sub_acc[first_id:stop_id], "row")
        unused, solved = solve_diagonal(given.astype(jnp.bfloat16), sub_lower[first_id:stop_id])
        sub_rows[depth_now] = solved
        per_node = levels + depth_now
        opening = SUB_NODES + sub_start[first_id]
        blocks = sub_lower[opening : opening + node_count * per_node].reshape(
            node_count, per_node, cols_here, rows_here
        )
        weights = low_pattern[sub_start[first_id] : sub_start[stop_id]].reshape(
            node_count, per_node
        )
        updates = jnp.einsum("npik,nkr->npir", blocks, solved, preferred_element_type=jnp.float32)
        updates = updates * weights[:, :, None, None]
        to_anc = to_anc + jnp.einsum("ea,eir->air", choose, jnp.sum(updates[:, :levels], 0))
        if depth_now > 0:
            table = jnp.asarray(local_routes(first_id, stop_id, depth_now, SUB_NODES))
            sub_acc = sub_acc + jnp.einsum(
                "tq,qir->tir", table, updates[:, levels:].reshape(-1, cols_here, R)
            )
    anc_acc = jnp.zeros((anc_count, cols_here, R), jnp.float32)
    anc_rows = {}
    for depth_now in reversed(range(levels)):
        first_id, stop_id = level_span(depth_now)
        node_count = stop_id - first_id
        joined = to_anc[first_id:stop_id] + first_layer * anc_acc[first_id:stop_id]
        reached = lax.psum(joined, ("gz", "row"))
        given = anc_rhs[first_id:stop_id].astype(jnp.float32) - reached
        unused, solved = solve_diagonal(given.astype(jnp.bfloat16), anc_lower[first_id:stop_id])
        anc_rows[depth_now] = solved
        if depth_now > 0:
            opening = anc_count + anc_start[first_id]
            blocks = anc_lower[opening : opening + node_count * depth_now].reshape(
                node_count, depth_now, cols_here, rows_here
            )
            updates = jnp.einsum(
                "npik,nkr->npir", blocks, solved, preferred_element_type=jnp.float32
            )
            table = jnp.asarray(local_routes(first_id, stop_id, depth_now, anc_count))
            anc_acc = anc_acc + jnp.einsum("tq,qir->tir", table, updates.reshape(-1, cols_here, R))
    anc_z_parts = []
    anc_out_parts = []
    for depth_now in range(levels):
        first_id, stop_id = level_span(depth_now)
        node_count = stop_id - first_id
        given = own_piece(anc_rows[depth_now])
        if depth_now > 0:
            z_sofar = jnp.concatenate(anc_z_parts, 0)
            table = local_routes(first_id, stop_id, depth_now, anc_count)[:first_id].T
            sources = jnp.einsum(
                "qa,akr->qkr",
                jnp.asarray(table, jnp.bfloat16),
                z_sofar,
                preferred_element_type=jnp.float32,
            )
            sources = sources.astype(jnp.bfloat16).reshape(node_count, depth_now, rows_here, R)
            opening = anc_count + anc_start[first_id]
            blocks = anc_upper[opening : opening + node_count * depth_now].reshape(
                node_count, depth_now, cols_here, rows_here
            )
            updates = jnp.einsum(
                "npik,npkr->npir", blocks, sources, preferred_element_type=jnp.float32
            )
            given = given - jnp.sum(updates, 1)
        summed = upper_sum(given)
        owned, solved = solve_diagonal(summed.astype(jnp.bfloat16), anc_upper[first_id:stop_id])
        anc_out_parts.append(owned)
        anc_z_parts.append(solved)
    anc_z_all = jnp.concatenate(anc_z_parts, 0)
    selected = jnp.einsum(
        "ea,akr->ekr", choose.astype(jnp.bfloat16), anc_z_all, preferred_element_type=jnp.float32
    )
    selected = selected.astype(jnp.bfloat16)
    sub_z_parts = []
    sub_out_parts = []
    for depth_now in range(SUB_LEVELS):
        first_id, stop_id = level_span(depth_now)
        node_count = stop_id - first_id
        per_node = levels + depth_now
        opening = SUB_NODES + sub_start[first_id]
        blocks = sub_upper[opening : opening + node_count * per_node].reshape(
            node_count, per_node, cols_here, rows_here
        )
        weights = up_pattern[sub_start[first_id] : sub_start[stop_id]].reshape(node_count, per_node)
        updates = jnp.einsum(
            "npik,pkr->npir", blocks[:, :levels], selected, preferred_element_type=jnp.float32
        )
        if depth_now > 0:
            z_sofar = sub_z_parts[0]
            table = local_routes(first_id, stop_id, depth_now, SUB_NODES)[:first_id].T
            sources = jnp.einsum(
                "qa,akr->qkr",
                jnp.asarray(table, jnp.bfloat16),
                z_sofar,
                preferred_element_type=jnp.float32,
            )
            sources = sources.astype(jnp.bfloat16).reshape(node_count, depth_now, rows_here, R)
            local_updates = jnp.einsum(
                "npik,npkr->npir", blocks[:, levels:], sources, preferred_element_type=jnp.float32
            )
            updates = jnp.concatenate([updates, local_updates], 1)
        change = jnp.sum(updates * weights[:, :, None, None], 1)
        summed = upper_sum(own_piece(sub_rows[depth_now]) - change)
        owned, solved = solve_diagonal(summed.astype(jnp.bfloat16), sub_upper[first_id:stop_id])
        sub_out_parts.append(owned)
        sub_z_parts.append(solved)
    return (jnp.concatenate(anc_out_parts, 0), jnp.concatenate(sub_out_parts, 0))


def solution(mesh):
    in_specs = (
        P(None, "col", "row"),
        P(None, "col", "row"),
        P("gz", "col", "row"),
        P("gz", "col", "row"),
        P(None, "col", None),
        P("gz", "col", None),
        P(),
        P("gz", None),
    )
    out_specs = (P(None, ("row", "col"), None), P("gz", ("row", "col"), None))
    return jax.shard_map(local, mesh=mesh, in_specs=in_specs, out_specs=out_specs, check_vma=False)
```

profile of v0, /device:TPU:0, one launch (start us, length us, event | category | flops | bytes accessed | tf_op | source)
XLA Modules:
  0.0 251.9 jit_solution(8480645708661849595)
XLA Ops:
  7.2 1.7 slice.67
  8.9 0.0 all-reduce.4.cloned.1.call-start
  9.0 0.6 copy-done.7
  9.6 0.6 fusion.35
  11.0 0.7 copy-done.6
  11.7 0.1 slice_reduce_fusion.2
  11.7 0.1 mul.92
  11.8 17.3 %all_gather.37 = bf16[2,1024,64]{1,2,0:T(8,128)(2,1)S(1)} all-gather(bf16[2,256,64]{1,2,0:T(8,128)(2,1)S(1)} %slice-done.3), channel_id=1, replica_groups=mesh['gz'=2,'row'=4,'col'=4] {'col'}, dimensions={1}, use_global_device_ids=true | all-gather | bytes 327680 | tf_op jit(solution)/shard_map/all_gather | solution.py:27
  29.1 22.6 %all_gather.39 = bf16[1,1024,256]{2,1,0:T(8,128)(2,1)S(1)} all-gather(bf16[1,256,256]{2,1,0:T(8,128)(2,1)S(1)} %slice-done.1), channel_id=1, replica_groups=mesh['gz'=2,'row'=4,'col'=4] {'col'}, dimensions={1}, use_global_device_ids=true | all-gather | bytes 655360 | tf_op jit(solution)/shard_map/all_gather | solution.py:26
  51.7 1.6 convolution_convert_fusion
  53.4 0.3 fusion
  53.7 0.3 copy-done.8
  54.0 0.9 fusion.27
  55.0 30.0 %all-reduce.4.cloned.1.call-done = f32[1,256,64]{1,0,2:T(1,128)} async-done(((f32[1,256,64]{1,0,2:T(1,128)}), f32[1,256,64]{1,0,2:T(1,128)}) %all-reduce.4.cloned.1.call-update) | async-done | bytes 65552 | tf_op jit(solution)/shard_map/psum | solution.py:84
  85.0 0.9 fusion.30
  85.9 13.5 %all_gather.38 = bf16[1,1024,64]{1,0,2:T(2,128)(2,1)S(1)} all-gather(bf16[1,256,64]{1,0,2:T(2,128)(2,1)S(1)} %fusion.30), channel_id=1, replica_groups=mesh['gz'=2,'row'=4,'col'=4] {'col'}, dimensions={1}, use_global_device_ids=true | all-gather | bytes 163840 | tf_op jit(solution)/shard_map/all_gather | solution.py:27
  99.4 0.2 convolution_convert_fusion.2
  99.6 0.9 fusion.7
  100.5 0.7 slice.87
  101.4 0.8 copy-done.3
  102.2 14.9 %all_gather.41 = bf16[1,1024,256]{2,1,0:T(8,128)(2,1)S(1)} all-gather(bf16[1,256,256]{2,1,0:T(8,128)(2,1)S(1)} %copy-done.3), channel_id=1, replica_groups=mesh['gz'=2,'row'=4,'col'=4] {'col'}, dimensions={1}, use_global_device_ids=true | all-gather | bytes 655360 | tf_op jit(solution)/shard_map/all_gather | solution.py:26
  117.1 16.3 %all_gather.43 = bf16[1,1024,256]{2,1,0:T(8,128)(2,1)S(1)} all-gather(bf16[1,256,256]{2,1,0:T(8,128)(2,1)S(1)} %copy-done.4), channel_id=1, replica_groups=mesh['gz'=2,'row'=4,'col'=4] {'col'}, dimensions={1}, use_global_device_ids=true | all-gather | bytes 655360 | tf_op jit(solution)/shard_map/all_gather | solution.py:26
  133.4 14.8 %all_gather.45 = bf16[1,1024,256]{2,1,0:T(8,128)(2,1)S(1)} all-gather(bf16[1,256,256]{2,1,0:T(8,128)(2,1)S(1)} %slice-done.2), channel_id=1, replica_groups=mesh['gz'=2,'row'=4,'col'=4] {'col'}, dimensions={1}, use_global_device_ids=true | all-gather | bytes 655360 | tf_op jit(solution)/shard_map/all_gather | solution.py:26
  148.2 0.1 slice_reduce_fusion.1
  148.3 0.1 mul.112
  148.4 0.1 copy.22
  148.5 2.8 %all-reduce.6.cloned.1.call-done = f32[1,256,64]{1,2,0:T(8,128)} async-done(((f32[1,256,64]{1,2,0:T(8,128)}), f32[1,256,64]{1,2,0:T(8,128)}) %all-reduce.6.cloned.1.call-update) | async-done | bytes 65552 | tf_op jit(solution)/shard_map/psum | solution.py:109
  151.3 0.8 subtract_convert_fusion
  152.1 13.9 %all_gather.40 = bf16[1,1024,64]{1,2,0:T(8,128)(2,1)S(1)} all-gather(bf16[1,256,64]{1,2,0:T(8,128)(2,1)S(1)} %subtract_convert_fusion), channel_id=1, replica_groups=mesh['gz'=2,'row'=4,'col'=4] {'col'}, dimensions={1}, use_global_device_ids=true | all-gather | bytes 163840 | tf_op jit(solution)/shard_map/all_gather | solution.py:27
  166.0 0.2 fusion.10
  166.2 11.5 %psum.37 = bf16[1,256,64]{1,2,0:T(8,128)(2,1)S(1)} all-reduce(f32[1,256,64]{1,2,0:T(8,128)S(1)} %fusion.10), channel_id=1, replica_groups=mesh['gz'=2,'row'=4,'col'=4] {'row'}, use_global_device_ids=true, to_apply=%region_4.5 | all-reduce | flops 16384 | bytes 98304 | tf_op jit(solution)/shard_map/psum | solution.py:37
  177.7 13.4 %all_gather.42 = bf16[1,1024,64]{1,2,0:T(8,128)(2,1)S(1)} all-gather(bf16[1,256,64]{1,2,0:T(8,128)(2,1)S(1)} %psum.37), channel_id=1, replica_groups=mesh['gz'=2,'row'=4,'col'=4] {'col'}, dimensions={1}, use_global_device_ids=true | all-gather | bytes 163840 | tf_op jit(solution)/shard_map/all_gather | solution.py:27
  191.1 0.2 fusion.13
  191.3 0.2 fusion.3
  191.5 10.7 %psum.38 = bf16[1,256,64]{1,2,0:T(8,128)(2,1)S(1)} all-reduce(f32[1,256,64]{1,2,0:T(8,128)S(1)} %fusion.3), channel_id=1, replica_groups=mesh['gz'=2,'row'=4,'col'=4] {'row'}, use_global_device_ids=true, to_apply=%region_5.6 | all-reduce | flops 16384 | bytes 98304 | tf_op jit(solution)/shard_map/psum | solution.py:37
  202.2 13.3 %all_gather.44 = bf16[1,1024,64]{1,2,0:T(8,128)(2,1)S(1)} all-gather(bf16[1,256,64]{1,2,0:T(8,128)(2,1)S(1)} %psum.38), channel_id=1, replica_groups=mesh['gz'=2,'row'=4,'col'=4] {'col'}, dimensions={1}, use_global_device_ids=true | all-gather | bytes 163840 | tf_op jit(solution)/shard_map/all_gather | solution.py:27
  215.5 0.2 fusion.11
  215.7 0.2 convolution_bitcast_fusion
  215.9 0.2 convolution_bitcast_fusion.1
  216.1 0.1 fusion.17
  216.3 11.9 %all-reduce.7 = bf16[2,256,64]{1,2,0:T(8,128)(2,1)S(1)} all-reduce(f32[2,256,64]{1,2,0:T(8,128)S(1)} %multiply_subtract_fusion), channel_id=1, replica_groups=mesh['gz'=2,'row'=4,'col'=4] {'row'}, use_global_device_ids=true, to_apply=%region_7.8 | all-reduce | flops 32768 | bytes 196608 | tf_op jit(solution)/shard_map/psum | solution.py:37
  228.2 14.0 %all_gather.46 = bf16[2,1024,64]{1,2,0:T(8,128)(2,1)S(1)} all-gather(bf16[2,256,64]{1,2,0:T(8,128)(2,1)S(1)} %all-reduce.7), channel_id=1, replica_groups=mesh['gz'=2,'row'=4,'col'=4] {'col'}, dimensions={1}, use_global_device_ids=true | all-gather | bytes 327680 | tf_op jit(solution)/shard_map/all_gather | solution.py:27
  242.1 0.1 dynamic-slice_bitcast_fusion.1
  242.2 0.1 dynamic-slice_bitcast_fusion.2
  242.3 1.5 fusion.36
  243.8 0.1 dynamic-slice_bitcast_fusion
  243.9 0.7 copy.24
  244.7 0.7 copy.23
  (40 shorter events, 0.4 us)
Async XLA Ops:
  7.2 44.6 %all-gather.3.cloned.1.call-start = ((), (), s32[]{:S(2)}) async-start(), calls=%async_computation | async-start | bytes 1310720 | tf_op jit(solution)/shard_map/all_gather | solution.py:26
  8.9 76.1 %all-reduce.4.cloned.1.call-start = ((), (), s32[]{:S(2)}) async-start(), calls=%async_computation.1 | async-start | bytes 131072 | tf_op jit(solution)/shard_map/psum | solution.py:84
  9.0 0.7 copy-start.7
  10.9 0.9 slice-start.3
  10.9 0.7 copy-start.6
  11.8 17.3 %slice-start.1 = ((bf16[8,256,256]{2,1,0:T(8,128)(2,1)}), bf16[1,256,256]{2,1,0:T(8,128)(2,1)S(1)}, s32[]{:S(2)}) async-start(bf16[8,256,256]{2,1,0:T(8,128)(2,1)} %param.13), calls=%async_computation.5 | async-start | bytes 262144 | tf_op jit(solution)/shard_map/slice | solution.py:85
  51.7 1.6 slice-start
  53.3 0.7 copy-start.8
  53.3 31.7 %slice-start.4 = ((bf16[3,256,64]{1,2,0:T(8,128)(2,1)}), bf16[1,256,64]{1,2,0:T(8,128)(2,1)S(1)}, s32[]{:S(2)}) async-start(bf16[3,256,64]{1,2,0:T(8,128)(2,1)} %param.16), calls=%async_computation.8 | async-start | bytes 65536 | tf_op jit(solution)/shard_map/slice | solution.py:82
  53.6 46.0 %copy-start = (bf16[8,256,256]{2,1,0:T(8,128)(2,1)S(1)}, bf16[8,256,256]{2,1,0:T(8,128)(2,1)}, u32[]{:S(2)}) copy-start(bf16[8,256,256]{2,1,0:T(8,128)(2,1)} %param.13) | copy-start | bytes 3145732
  54.0 46.5 %copy-start.1 = (bf16[8,256,256]{2,1,0:T(8,128)(2,1)S(1)}, bf16[8,256,256]{2,1,0:T(8,128)(2,1)}, u32[]{:S(2)}) copy-start(bf16[8,256,256]{2,1,0:T(8,128)(2,1)} %param.14) | copy-start | bytes 3145732
  54.9 96.3 %all-reduce.6.cloned.1.call-start = ((), (), s32[]{:S(2)}) async-start(), calls=%async_computation.2 | async-start | bytes 131072 | tf_op jit(solution)/shard_map/psum | solution.py:109
  100.5 141.8 %all-gather.5.cloned.1.call-start = ((), (), s32[]{:S(2)}) async-start(), calls=%async_computation.3 | async-start | bytes 1310720 | tf_op jit(solution)/shard_map/all_gather | solution.py:26
  101.3 0.9 copy-start.3
  102.2 14.9 %copy-start.4 = (bf16[1,256,256]{2,1,0:T(8,128)(2,1)S(1)}, bf16[1,256,256]{2,1,0:T(8,128)(2,1)}, u32[]{:S(2)}) copy-start(bf16[1,256,256]{2,1,0:T(8,128)(2,1)} %param.12) | copy-start | bytes 393220
  117.1 16.3 %slice-start.2 = ((bf16[8,256,256]{2,1,0:T(8,128)(2,1)}), bf16[1,256,256]{2,1,0:T(8,128)(2,1)S(1)}, s32[]{:S(2)}) async-start(bf16[8,256,256]{2,1,0:T(8,128)(2,1)} %param.14), calls=%async_computation.6 | async-start | bytes 262144 | tf_op jit(solution)/shard_map/slice | solution.py:186
  133.4 17.9 %copy-start.5 = (bf16[1,256,64]{1,2,0:T(8,128)(2,1)S(1)}, bf16[1,256,64]{1,2,0:T(8,128)(2,1)}, u32[]{:S(2)}) copy-start(bf16[1,256,64]{1,2,0:T(8,128)(2,1)} %param.15) | copy-start | bytes 98308
  148.2 43.1 %copy-start.2 = (bf16[8,256,256]{2,1,0:T(8,128)(2,1)S(1)}, bf16[8,256,256]{2,1,0:T(8,128)(2,1)}, u32[]{:S(2)}) copy-start(bf16[8,256,256]{2,1,0:T(8,128)(2,1)} %param.14) | copy-start | bytes 3145732
Sparse Core Ops, SparseCore 0:
  9.5 40.4 all-gather.2
  55.0 29.9 all-reduce.3
  100.6 50.5 all-reduce.5
  152.7 27.7 all-gather.4
where the time goes:
time: 253 us; the launch traced here: 252 us
  blocking collectives  188 us (74%)
  waiting for transfers between devices  32.9 us (13%)
  between operations  14.7 us (6%)
  local copies, waits for them, and re-layouts  7.11 us (3%)
  matrix products  6.59 us (3%)
    all_gather x6, blocking collectives, solve_diagonal(): whole_res = lax.all_gather(residual, 'col', axis=1, tiled=True)  85.3 us
    all_gather x4, blocking collectives, solve_diagonal(): whole_blocks = lax.all_gather(blocks, 'col', axis=1, tiled=True)  68.6 us
    psum x3, blocking collectives, upper_sum(): return lax.psum(values, 'row')  34 us
    psum x1, waiting for transfers between devices, local(): given = given - lax.psum(sub_acc[first_id:stop_id], 'row')  30 us
  transfers between devices with their start and end apart: 4, of which 2 were waited for; matrix products, arithmetic and copies ran while one was open for 2% of the time, Pallas kernels for 0%

commit v1 on v0

--- a/solution.py
+++ b/solution.py
@@ -1,12 +1,22 @@
+import functools
 import jax
 import jax.numpy as jnp
 import numpy as np
 from jax import lax
 from jax.sharding import PartitionSpec as P
+from jax.lax import all_gather
 
 R = 64
 SUB_LEVELS = 2
 SUB_NODES = 3
+
+
+def scan_threads(vec, axis_name):
+    odd = all_gather(vec, axis_name)
+    return jnp.sum(odd, 0)
+
+
+task_search = functools.partial(scan_threads, axis_name="row")
 
 
 def level_span(depth_now):
@@ -81,7 +91,7 @@
         node_count = stop_id - first_id
         given = sub_rhs[first_id:stop_id].astype(jnp.float32)
         if depth_now + 1 < SUB_LEVELS:
-            given = given - lax.psum(sub_acc[first_id:stop_id], "row")
+            given = given - task_search(sub_acc[first_id:stop_id])
         unused, solved = solve_diagonal(given.astype(jnp.bfloat16), sub_lower[first_id:stop_id])
         sub_rows[depth_now] = solved
         per_node = levels + depth_now

time: 253 us -> 229 us (0.905)
  waiting for transfers between devices: 32.9 us -> 3.96 us
  blocking collectives: 188 us -> 194 us
    psum x1 -> x0, waiting for transfers between devices: 30 us -> none  [local(): given = given - lax.psum(sub_acc[first_id:stop_id], 'row')]
    all_gather x0 -> x1, blocking collectives: none -> 5.91 us  [scan_threads(): odd = all_gather(vec, axis_name)]
  transfers between devices with their start and end apart: 4 -> 3, of which waited for: 2 -> 1; matrix products, arithmetic and copies ran while one was open for 2% -> 2% of each run, Pallas kernels for 0% -> 0%
where the time goes in v1:
time: 229 us
  blocking collectives  194 us (85%)
  between operations  14.7 us (6%)
  local copies, waits for them, and re-layouts  8.24 us (4%)
  matrix products  5.93 us (3%)
  waiting for transfers between devices  3.96 us (2%)
    all_gather x6, blocking collectives, solve_diagonal(): whole_res = lax.all_gather(residual, 'col', axis=1, tiled=True)  85.7 us
    all_gather x4, blocking collectives, solve_diagonal(): whole_blocks = lax.all_gather(blocks, 'col', axis=1, tiled=True)  68.5 us
    psum x3, blocking collectives, upper_sum(): return lax.psum(values, 'row')  34 us
    all_gather x1, blocking collectives, scan_threads(): odd = all_gather(vec, axis_name)  5.91 us
  transfers between devices with their start and end apart: 3, of which 1 were waited for; matrix products, arithmetic and copies ran while one was open for 2% of the time, Pallas kernels for 0%

profile of v1, /device:TPU:0, one launch (start us, length us, event | category | flops | bytes accessed | tf_op | source)
XLA Modules:
  0.0 228.7 jit_solution(2245774289420561933)
XLA Ops:
  7.2 1.7 slice.67
  9.0 0.6 copy-done.8
  9.6 0.6 fusion.33
  11.0 0.7 copy-done.7
  11.6 0.1 slice_reduce_fusion.2
  11.7 0.1 mul.92
  11.8 0.8 slice-done.3
  12.6 17.5 %all_gather.43 = bf16[2,1024,64]{1,2,0:T(8,128)(2,1)S(1)} all-gather(bf16[2,256,64]{1,2,0:T(8,128)(2,1)S(1)} %slice-done.3), channel_id=1, replica_groups=mesh['gz'=2,'row'=4,'col'=4] {'col'}, dimensions={1}, use_global_device_ids=true | all-gather | bytes 327680 | tf_op jit(solution)/shard_map/all_gather | solution.py:37
  30.1 22.7 %all_gather.47 = bf16[1,1024,256]{2,1,0:T(8,128)(2,1)S(1)} all-gather(bf16[1,256,256]{2,1,0:T(8,128)(2,1)S(1)} %slice-done.1), channel_id=1, replica_groups=mesh['gz'=2,'row'=4,'col'=4] {'col'}, dimensions={1}, use_global_device_ids=true | all-gather | bytes 655360 | tf_op jit(solution)/shard_map/all_gather | solution.py:36
  52.9 1.6 convolution_convert_fusion
  54.5 0.3 fusion
  54.8 0.6 copy-done.9
  55.4 0.3 fusion.26
  55.7 5.9 %all-gather = f32[4,256,64]{1,2,0:T(8,128)S(1)} all-gather(f32[1,256,64]{1,2,0:T(8,128)S(1)} %copy.24), channel_id=2, replica_groups=mesh['gz'=2,'row'=4,'col'=4] {'row'}, dimensions={0}, use_global_device_ids=true | all-gather | bytes 327680 | tf_op jit(solution)/shard_map/all_gather | solution.py:15
  61.7 13.7 %all_gather.46 = bf16[1,1024,64]{1,2,0:T(8,128)(2,1)S(1)} all-gather(bf16[1,256,64]{1,2,0:T(8,128)(2,1)S(1)} %fusion.29), channel_id=1, replica_groups=mesh['gz'=2,'row'=4,'col'=4] {'col'}, dimensions={1}, use_global_device_ids=true | all-gather | bytes 163840 | tf_op jit(solution)/shard_map/all_gather | solution.py:37
  75.3 0.2 convolution_convert_fusion.2
  75.5 0.9 fusion.7
  76.4 0.0 all-gather.6.cloned.1.call-start
  76.5 0.7 slice.87
  77.3 0.8 copy-done.4
  78.2 15.0 %all_gather.49 = bf16[1,1024,256]{2,1,0:T(8,128)(2,1)S(1)} all-gather(bf16[1,256,256]{2,1,0:T(8,128)(2,1)S(1)} %copy-done.4), channel_id=1, replica_groups=mesh['gz'=2,'row'=4,'col'=4] {'col'}, dimensions={1}, use_global_device_ids=true | all-gather | bytes 655360 | tf_op jit(solution)/shard_map/all_gather | solution.py:36
  93.2 15.8 %all_gather.51 = bf16[1,1024,256]{2,1,0:T(8,128)(2,1)S(1)} all-gather(bf16[1,256,256]{2,1,0:T(8,128)(2,1)S(1)} %copy-done.5), channel_id=1, replica_groups=mesh['gz'=2,'row'=4,'col'=4] {'col'}, dimensions={1}, use_global_device_ids=true | all-gather | bytes 655360 | tf_op jit(solution)/shard_map/all_gather | solution.py:36
  108.9 15.0 %all_gather.53 = bf16[1,1024,256]{2,1,0:T(8,128)(2,1)S(1)} all-gather(bf16[1,256,256]{2,1,0:T(8,128)(2,1)S(1)} %slice-done.2), channel_id=1, replica_groups=mesh['gz'=2,'row'=4,'col'=4] {'col'}, dimensions={1}, use_global_device_ids=true | all-gather | bytes 655360 | tf_op jit(solution)/shard_map/all_gather | solution.py:36
  123.9 0.1 slice_reduce_fusion.1
  124.0 0.1 mul.112
  124.1 0.1 copy.27
  124.2 3.9 %all-reduce.3.cloned.1.call-done = f32[1,256,64]{1,2,0:T(8,128)} async-done(((f32[1,256,64]{1,2,0:T(8,128)}), f32[1,256,64]{1,2,0:T(8,128)}) %all-reduce.3.cloned.1.call-update) | async-done | bytes 65552 | tf_op jit(solution)/shard_map/psum | solution.py:119
  128.1 0.8 subtract_convert_fusion
  129.0 13.9 %all_gather.48 = bf16[1,1024,64]{1,2,0:T(8,128)(2,1)S(1)} all-gather(bf16[1,256,64]{1,2,0:T(8,128)(2,1)S(1)} %subtract_convert_fusion), channel_id=1, replica_groups=mesh['gz'=2,'row'=4,'col'=4] {'col'}, dimensions={1}, use_global_device_ids=true | all-gather | bytes 163840 | tf_op jit(solution)/shard_map/all_gather | solution.py:37
  142.8 0.2 fusion.10
  143.0 11.5 %psum.29 = bf16[1,256,64]{1,2,0:T(8,128)(2,1)S(1)} all-reduce(f32[1,256,64]{1,2,0:T(8,128)S(1)} %fusion.10), channel_id=1, replica_groups=mesh['gz'=2,'row'=4,'col'=4] {'row'}, use_global_device_ids=true, to_apply=%region_4.5 | all-reduce | flops 16384 | bytes 98304 | tf_op jit(solution)/shard_map/psum | solution.py:47
  154.5 13.4 %all_gather.50 = bf16[1,1024,64]{1,2,0:T(8,128)(2,1)S(1)} all-gather(bf16[1,256,64]{1,2,0:T(8,128)(2,1)S(1)} %psum.29), channel_id=1, replica_groups=mesh['gz'=2,'row'=4,'col'=4] {'col'}, dimensions={1}, use_global_device_ids=true | all-gather | bytes 163840 | tf_op jit(solution)/shard_map/all_gather | solution.py:37
  167.9 0.2 fusion.13
  168.1 0.2 fusion.3
  168.3 10.7 %psum.30 = bf16[1,256,64]{1,2,0:T(8,128)(2,1)S(1)} all-reduce(f32[1,256,64]{1,2,0:T(8,128)S(1)} %fusion.3), channel_id=1, replica_groups=mesh['gz'=2,'row'=4,'col'=4] {'row'}, use_global_device_ids=true, to_apply=%region_5.6 | all-reduce | flops 16384 | bytes 98304 | tf_op jit(solution)/shard_map/psum | solution.py:47
  179.0 13.4 %all_gather.52 = bf16[1,1024,64]{1,2,0:T(8,128)(2,1)S(1)} all-gather(bf16[1,256,64]{1,2,0:T(8,128)(2,1)S(1)} %psum.30), channel_id=1, replica_groups=mesh['gz'=2,'row'=4,'col'=4] {'col'}, dimensions={1}, use_global_device_ids=true | all-gather | bytes 163840 | tf_op jit(solution)/shard_map/all_gather | solution.py:37
  192.3 0.2 fusion.11
  192.6 0.2 convolution_bitcast_fusion
  192.7 0.2 convolution_bitcast_fusion.1
  193.0 0.1 fusion.17
  193.1 11.9 %all-reduce.4 = bf16[2,256,64]{1,2,0:T(8,128)(2,1)S(1)} all-reduce(f32[2,256,64]{1,2,0:T(8,128)S(1)} %multiply_subtract_fusion), channel_id=1, replica_groups=mesh['gz'=2,'row'=4,'col'=4] {'row'}, use_global_device_ids=true, to_apply=%region_7.8 | all-reduce | flops 32768 | bytes 196608 | tf_op jit(solution)/shard_map/psum | solution.py:47
  205.0 14.0 %all_gather.54 = bf16[2,1024,64]{1,2,0:T(8,128)(2,1)S(1)} all-gather(bf16[2,256,64]{1,2,0:T(8,128)(2,1)S(1)} %all-reduce.4), channel_id=1, replica_groups=mesh['gz'=2,'row'=4,'col'=4] {'col'}, dimensions={1}, use_global_device_ids=true | all-gather | bytes 327680 | tf_op jit(solution)/shard_map/all_gather | solution.py:37
  218.9 0.1 dynamic-slice_bitcast_fusion.1
  219.0 0.1 dynamic-slice_bitcast_fusion.2
  219.1 1.5 fusion.34
  220.6 0.1 dynamic-slice_bitcast_fusion
  220.7 0.7 copy.29
  221.5 0.7 copy.28
  (40 shorter events, 0.3 us)
Async XLA Ops:
  7.2 45.7 %all-gather.4.cloned.1.call-start = ((), (), s32[]{:S(2)}) async-start(), calls=%async_computation | async-start | bytes 1310720 | tf_op jit(solution)/shard_map/all_gather | solution.py:36
  8.9 119.2 %all-reduce.3.cloned.1.call-start = ((), (), s32[]{:S(2)}) async-start(), calls=%async_computation.1 | async-start | bytes 131072 | tf_op jit(solution)/shard_map/psum | solution.py:119
  9.0 0.7 copy-start.8
  10.9 0.7 copy-start.7
  11.8 0.8 slice-start.3
  12.6 17.5 %slice-start.1 = ((bf16[8,256,256]{2,1,0:T(8,128)(2,1)}), bf16[1,256,256]{2,1,0:T(8,128)(2,1)S(1)}, s32[]{:S(2)}) async-start(bf16[8,256,256]{2,1,0:T(8,128)(2,1)} %param.13), calls=%async_computation.4 | async-start | bytes 262144 | tf_op jit(solution)/shard_map/slice | solution.py:95
  52.9 1.6 slice-start
  54.8 0.7 copy-start.9
  54.8 6.9 %copy-start.3 = (bf16[3,256,64]{1,2,0:T(8,128)(2,1)S(1)}, bf16[3,256,64]{1,2,0:T(8,128)(2,1)}, u32[]{:S(2)}) copy-start(bf16[3,256,64]{1,2,0:T(8,128)(2,1)} %param.16) | copy-start | bytes 294916
  55.4 20.1 %copy-start = (bf16[8,256,256]{2,1,0:T(8,128)(2,1)S(1)}, bf16[8,256,256]{2,1,0:T(8,128)(2,1)}, u32[]{:S(2)}) copy-start(bf16[8,256,256]{2,1,0:T(8,128)(2,1)} %param.13) | copy-start | bytes 3145732
  55.7 20.8 %copy-start.1 = (bf16[8,256,256]{2,1,0:T(8,128)(2,1)S(1)}, bf16[8,256,256]{2,1,0:T(8,128)(2,1)}, u32[]{:S(2)}) copy-start(bf16[8,256,256]{2,1,0:T(8,128)(2,1)} %param.14) | copy-start | bytes 3145732
  76.4 142.7 %all-gather.6.cloned.1.call-start = ((), (), s32[]{:S(2)}) async-start(), calls=%async_computation.2 | async-start | bytes 1310720 | tf_op jit(solution)/shard_map/all_gather | solution.py:36
  77.3 0.9 copy-start.4
  78.2 15.0 %copy-start.5 = (bf16[1,256,256]{2,1,0:T(8,128)(2,1)S(1)}, bf16[1,256,256]{2,1,0:T(8,128)(2,1)}, u32[]{:S(2)}) copy-start(bf16[1,256,256]{2,1,0:T(8,128)(2,1)} %param.12) | copy-start | bytes 393220
  93.2 15.8 %slice-start.2 = ((bf16[8,256,256]{2,1,0:T(8,128)(2,1)}), bf16[1,256,256]{2,1,0:T(8,128)(2,1)S(1)}, s32[]{:S(2)}) async-start(bf16[8,256,256]{2,1,0:T(8,128)(2,1)} %param.14), calls=%async_computation.5 | async-start | bytes 262144 | tf_op jit(solution)/shard_map/slice | solution.py:196
  108.9 19.2 %copy-start.6 = (bf16[1,256,64]{1,2,0:T(8,128)(2,1)S(1)}, bf16[1,256,64]{1,2,0:T(8,128)(2,1)}, u32[]{:S(2)}) copy-start(bf16[1,256,64]{1,2,0:T(8,128)(2,1)} %param.15) | copy-start | bytes 98308
  123.9 44.1 %copy-start.2 = (bf16[8,256,256]{2,1,0:T(8,128)(2,1)S(1)}, bf16[8,256,256]{2,1,0:T(8,128)(2,1)}, u32[]{:S(2)}) copy-start(bf16[8,256,256]{2,1,0:T(8,128)(2,1)} %param.14) | copy-start | bytes 3145732
Sparse Core Ops, SparseCore 0:
  9.5 40.6 all-gather.3
  76.5 51.5 all-reduce.2
  129.7 27.7 all-gather.5
